TPU v7x, 32 devices: a whole 2x2x4 slice. The times are simulated.
32 devices in a mesh: ctx: 8 (over z, y), grp: 4 (over x, core).
Axes of the slice: x: 2, y: 2, z: 4, core: 2. Of those that a mesh axis runs over, the one named last changes fastest.
Arguments:
- tokens: bfloat16 [4, 512, 8192], P('grp', 'ctx'), may hold values from -6 to 6
- queries: bfloat16 [4, 512, 4096], P('grp', 'ctx'), may hold values from -32 to 32
- key_value_weight: bfloat16 [8192, 1024], P('grp'), may hold values from -0.0625 to 0.0625
- adapter_down_weight: bfloat16 [8192, 128], P('grp'), may hold values from -0.0625 to 0.0625
- adapter_up_weight: bfloat16 [2, 64, 512], replicated, may hold values from -0.75 to 0.75
- tile_request_mask: int32 [4, 4, 4], P('grp'), may hold values 0 or 1
- lengths: int32 [4], P('grp'), may hold values from 128 to 512, as said below
- page_lookup_table: int32 [4, 128], P(None, 'ctx'), may hold values from 0 to 63, as said below
Outputs:
- attended: bfloat16 [4, 512, 4096], P('grp', 'ctx')
- decode_cache: bfloat16 [4, 128, 4, 1024], P('grp', 'ctx')
Inputs may be any that keep to these rules, and one draw needn't show every extreme that they name: `page_lookup_table`: pages of positions held by one index of ctx go to decode-cache rows of that same index. Every decode group receives exactly 16 pages into distinct slots from the pages of each index of ctx. From the pages of one rollout on one index of ctx, at most max(2, ceil(4)) go to one group, and exactly that many to some group. `lengths`: some rollout has all 512 positions live.
All inputs are finite; a program needn't handle non-finite values. No bound on the sum of `tile_request_mask` on one device may be relied on, other than what follows from the above.
Results may differ from a plain program's by a relative error of at most 0.028.
Values may be sent and summed in bfloat16 or wider, within the bound.
A program may use at most 64 MiB of HBM per device.

v0:
```python
import jax
import jax.numpy as jnp
from jax import lax
from jax.sharding import PartitionSpec as P

HEAD_SIZE = 128
HQ = 32
KEY_VALUE_HEADS = 4
PAGE = 4
TILE = 128


THETA = 500000.0
ADAPTER_SCALE = 0.5


def rotate(key_rows, token_positions):
    half_split = HEAD_SIZE // 2
    freq = THETA ** (-(2.0 * jnp.arange(half_split, dtype=jnp.float32)) / HEAD_SIZE)
    angle = token_positions.astype(jnp.float32)[:, None] * freq[None, :]
    cosine = jnp.cos(angle)[:, None, :]
    sine = jnp.sin(angle)[:, None, :]
    first = key_rows[..., :half_split]
    second = key_rows[..., half_split:]
    return jnp.concatenate([first * cosine - second * sine, second * cosine + first * sine], -1)


def send_pages(own, page_lookup_table, groups):
    column_width = own.shape[1]
    ppd = own.shape[0] // PAGE
    most = max(2, -(-ppd // groups))
    me = lax.axis_index("grp")
    dest = page_lookup_table // ppd
    slot = page_lookup_table % ppd
    earlier = jnp.arange(ppd)[:, None] > jnp.arange(ppd)[None, :]
    same = dest[:, :, None] == dest[:, None, :]
    order = jnp.sum(same & earlier[None], axis=2)
    my_dest = lax.dynamic_index_in_dim(dest, me, 0, keepdims=False)
    my_order = lax.dynamic_index_in_dim(order, me, 0, keepdims=False)
    pick = (my_dest[None, None, :] == jnp.arange(groups)[:, None, None]) & (
        my_order[None, None, :] == jnp.arange(most)[None, :, None]
    )
    pages = own.reshape(ppd, PAGE * column_width)
    outgoing = jnp.einsum(
        "gck,kf->gcf", pick.astype(jnp.bfloat16), pages, preferred_element_type=jnp.float32
    ).astype(jnp.bfloat16)
    incoming = lax.all_to_all(outgoing, "grp", split_axis=0, concat_axis=0, tiled=True)
    place = (
        (dest[None, :, None, :] == me)
        & (order[None, :, None, :] == jnp.arange(most)[None, None, :, None])
        & (slot[None, :, None, :] == jnp.arange(ppd)[:, None, None, None])
    )
    place = jnp.any(place, axis=3).reshape(ppd, groups * most)
    cache = jnp.dot(
        place.astype(jnp.bfloat16),
        incoming.reshape(groups * most, PAGE * column_width),
        preferred_element_type=jnp.float32,
    )
    return cache.astype(jnp.bfloat16).reshape(1, ppd, PAGE, column_width)


def local(
    tokens,
    queries,
    key_value_weight,
    adapter_down_weight,
    adapter_up_weight,
    tile_request_mask,
    lengths,
    page_lookup_table,
):
    groups = lax.axis_size("grp")
    tok = tokens.shape[1]
    column_width = key_value_weight.shape[1]
    half_split = column_width // 2
    rank_count = adapter_up_weight.shape[1]
    group = HQ // KEY_VALUE_HEADS
    ctx_pos = lax.axis_index("ctx")
    token_positions = ctx_pos * tok + jnp.arange(tok, dtype=jnp.int32)
    mixed_output = lax.all_to_all(tokens[0], "grp", split_axis=1, concat_axis=0, tiled=True)
    summed_output = lax.psum_scatter(
        jnp.concatenate(
            [
                jnp.dot(mixed_output, key_value_weight, preferred_element_type=jnp.float32),
                jnp.dot(mixed_output, adapter_down_weight, preferred_element_type=jnp.float32),
            ],
            1,
        ).astype(jnp.bfloat16),
        "grp",
        scatter_dimension=0,
        tiled=True,
    ).astype(jnp.float32)
    low_rank_state = summed_output[:, column_width:].astype(jnp.bfloat16)
    key_rows = summed_output[:, :half_split] + ADAPTER_SCALE * jnp.dot(
        low_rank_state[:, :rank_count], adapter_up_weight[0], preferred_element_type=jnp.float32
    )
    value_rows = summed_output[:, half_split:column_width] + ADAPTER_SCALE * jnp.dot(
        low_rank_state[:, rank_count:], adapter_up_weight[1], preferred_element_type=jnp.float32
    )
    key_rows = rotate(key_rows.reshape(tok, KEY_VALUE_HEADS, HEAD_SIZE), token_positions).reshape(
        tok, half_split
    )
    own = jnp.concatenate([key_rows, value_rows], 1).astype(jnp.bfloat16)
    decode_cache = send_pages(own, page_lookup_table, groups)
    query_heads = queries[0].reshape(tok, KEY_VALUE_HEADS, group, HEAD_SIZE)
    scale = 1.0 / HEAD_SIZE**0.5
    tiles = tile_request_mask.shape[1]
    tile_ids = jnp.arange(tiles, dtype=jnp.int32)
    query_tile = token_positions // TILE
    query_onehot = (query_tile[:, None] == tile_ids[None, :]).astype(jnp.float32)
    live_rows = jnp.dot(query_onehot, tile_request_mask[0].astype(jnp.float32))
    length = lengths[0]
    initial = (
        jnp.full((KEY_VALUE_HEADS, group, tok, 1), -1e30, jnp.float32),
        jnp.zeros((KEY_VALUE_HEADS, group, tok, 1), jnp.float32),
        jnp.zeros((KEY_VALUE_HEADS, group, tok, HEAD_SIZE), jnp.float32),
    )
    state = initial
    piece = lax.all_gather(own, "ctx", axis=0, tiled=True)
    count = piece.shape[0]
    blk = 512
    blocks = piece.reshape(count // blk, blk, column_width)

    def inner(carry, item):
        offset, block = item
        peak, total, acc = carry
        kpos = offset * blk + jnp.arange(blk, dtype=jnp.int32)
        key_block = block[:, :half_split].reshape(blk, KEY_VALUE_HEADS, HEAD_SIZE)
        value_block = (
            block[:, half_split:].reshape(blk, KEY_VALUE_HEADS, HEAD_SIZE).astype(jnp.float32)
        )
        score = (
            jnp.einsum("qhgd,khd->hgqk", query_heads, key_block, preferred_element_type=jnp.float32)
            * scale
        )
        key_tile = kpos // TILE
        key_onehot = (key_tile[:, None] == tile_ids[None, :]).astype(jnp.float32)
        live = jnp.dot(live_rows, key_onehot.T) > 0.5
        live = live | (query_tile[:, None] == key_tile[None, :])
        allowed = (kpos[None, :] <= token_positions[:, None]) & (kpos[None, :] >= 0) & live & (
            kpos[None, :] < length
        ) | (kpos[None, :] == token_positions[:, None])
        masked = jnp.where(allowed, score, -1e30)
        new_peak = jnp.maximum(peak, jnp.max(masked, axis=-1, keepdims=True))
        expo = jnp.where(allowed, jnp.exp(masked - new_peak), 0.0)
        factor = jnp.exp(peak - new_peak)
        total = total * factor + jnp.sum(expo, axis=-1, keepdims=True)
        acc = acc * factor + jnp.einsum(
            "hgqk,khd->hgqd", expo, value_block, preferred_element_type=jnp.float32
        )
        return ((new_peak, total, acc), None)

    offsets = jnp.arange(count // blk, dtype=jnp.int32)
    state, _ = lax.scan(inner, state, (offsets, blocks))
    peak, total, acc = state
    out = acc / total
    out = jnp.transpose(out, (2, 0, 1, 3)).reshape(tok, HQ * HEAD_SIZE)
    out = jnp.where((token_positions < length)[:, None], out, 0.0)
    attended = out.astype(jnp.bfloat16)[None]
    return (attended, decode_cache)


def solution(mesh):
    in_specs = (
        P("grp", "ctx", None),
        P("grp", "ctx", None),
        P("grp", None),
        P("grp", None),
        P(),
        P("grp", None, None),
        P("grp"),
        P(None, "ctx"),
    )
    out_specs = (P("grp", "ctx", None), P("grp", "ctx", None, None))
    return jax.shard_map(local, mesh=mesh, in_specs=in_specs, out_specs=out_specs, check_vma=False)
```

profile of v0, /device:TPU:0, one launch (start us, length us, event | category | flops | bytes accessed | tf_op | source)
XLA Modules:
  0.0 115.5 jit_solution(12051520847819461086)
XLA Ops:
  7.2 0.0 copy-start
  7.2 1.9 %all_to_all.17 = bf16[64,4,2048]{2,1,0:T(4,128)(2,1)S(1)} reshape(bf16[1,64,8192]{2,1,0:T(8,128)(2,1)} %param.8) | data formatting | bytes 2097152 | tf_op jit(solution)/shard_map/all_to_all | solution.py:80
  9.1 1.5 %copy.31 = bf16[64,4,2048]{2,0,1:T(8,128)(2,1)} copy(bf16[64,4,2048]{2,1,0:T(4,128)(2,1)S(1)} %all_to_all.17) | data formatting | bytes 2097152 | tf_op jit(solution)/shard_map/all_to_all | solution.py:80
  10.6 4.2 %all-to-all-start = ((bf16[64,4,2048]{2,0,1:T(8,128)(2,1)}), bf16[64,4,2048]{2,0,1:T(8,128)(2,1)S(1)}, u32[]{:S(2)}, u32[]{:S(2)}) async-start(bf16[64,4,2048]{2,0,1:T(8,128)(2,1)} %copy.31), calls=%async_computation | async-start | bytes 2097152 | tf_op jit(solution)/shard_map/all_to_all | solution.py:80
  14.8 0.0 reduce-scatter.2.cloned.1.call-start
  14.9 14.4 %all-to-all-done = bf16[64,4,2048]{2,0,1:T(8,128)(2,1)S(1)} async-done(((bf16[64,4,2048]{2,0,1:T(8,128)(2,1)}), bf16[64,4,2048]{2,0,1:T(8,128)(2,1)S(1)}, u32[]{:S(2)}, u32[]{:S(2)}) %all-to-all-start) | async-done | bytes 1048608 | tf_op jit(solution)/shard_map/all_to_all | solution.py:80
  29.3 0.0 copy-done
  29.3 0.4 convolution_convert_fusion.2
  29.7 0.0 copy-start.3
  29.8 0.0 copy-start.2
  29.8 0.0 copy-start.1
  29.8 3.5 %convolution_convert_fusion.1 = bf16[256,1024]{1,0:T(8,128)(2,1)S(1)} fusion(bf16[256,2048]{1,0:T(8,128)(2,1)S(1)} %bitcast.71, bf16[2048,1024]{1,0:T(8,128)(2,1)} %param.10), kind=kOutput, calls=%fused_computation.15 | convolution fusion | flops 1074003968 | bytes 5767168 | tf_op jit(solution)/shard_map/dot_general | solution.py:84
  33.3 0.0 copy-start.4
  33.3 0.9 pad_maximum_fusion
  34.2 0.0 reduce-scatter.2.cloned.1.call-update
  34.2 0.0 all-gather.2.cloned.1.call-start
  34.9 0.0 copy-done.3
  35.0 0.2 convert_reduce_fusion
  35.2 0.2 multiply_cosine_fusion
  35.4 22.0 %reduce-scatter.2.cloned.1.call-done = bf16[64,1152]{1,0:T(8,128)(2,1)} async-done(((bf16[256,1152]{1,0:T(8,128)(2,1)}), bf16[64,1152]{1,0:T(8,128)(2,1)}) %reduce-scatter.2.cloned.1.call-update) | async-done | bytes 147472 | tf_op jit(solution)/shard_map/reduce_scatter | solution.py:81
  57.4 0.9 convert_element_type.53
  58.4 0.0 copy-done.2
  58.4 0.9 fusion.12
  59.3 0.2 multiply_subtract_fusion
  59.5 0.1 pad_maximum_fusion.1
  59.6 0.9 fusion.11
  60.5 0.7 maximum_convert_fusion
  61.2 0.0 all-gather.2.cloned.1.call-update
  61.2 0.0 copy-done.1
  61.2 0.1 copy.45
  61.4 0.4 and_reduce_fusion
  61.8 0.4 fusion.16
  62.2 1.0 reshape.298
  63.2 0.8 convolution_convert_fusion
  64.1 3.3 %all-to-all-start.1 = ((bf16[4,4,4096]{2,1,0:T(4,128)(2,1)}), bf16[4,4,4096]{2,1,0:T(4,128)(2,1)S(1)}, u32[]{:S(2)}, u32[]{:S(2)}) async-start(bf16[4,4,4096]{2,1,0:T(4,128)(2,1)} %convolution_convert_fusion), calls=%async_computation.2 | async-start | bytes 262144 | tf_op jit(solution)/shard_map/all_to_all | solution.py:47
  67.4 4.6 %all-to-all-done.1 = bf16[4,4,4096]{2,1,0:T(4,128)(2,1)S(1)} async-done(((bf16[4,4,4096]{2,1,0:T(4,128)(2,1)}), bf16[4,4,4096]{2,1,0:T(4,128)(2,1)S(1)}, u32[]{:S(2)}, u32[]{:S(2)}) %all-to-all-start.1) | async-done | bytes 131104 | tf_op jit(solution)/shard_map/all_to_all | solution.py:47
  72.0 0.2 fusion
  72.2 0.7 reshape.295
  73.0 28.6 %all-gather.2.cloned.1.call-done = bf16[512,1024]{1,0:T(8,128)(2,1)} async-done(((bf16[64,1024]{1,0:T(8,128)(2,1)}), bf16[512,1024]{1,0:T(8,128)(2,1)}) %all-gather.2.cloned.1.call-update) | async-done | bytes 1048592 | tf_op jit(solution)/shard_map/all_gather | solution.py:119
  101.6 1.3 %fusion.49 = (bf16[512,512]{1,0:T(8,128)(2,1)S(1)}, bf16[512,512]{1,0:T(8,128)(2,1)S(1)}) fusion(bf16[512,1024]{1,0:T(8,128)(2,1)} %all-gather.2.cloned.1.call-done), kind=kLoop, calls=%fused_computation.99 | loop fusion | bytes 2097152 | tf_op jit(solution)/shard_map/while/body/eval_jaxpr/slice | solution.py:130
  102.9 0.1 reshape.293
  103.0 0.1 reshape.292
  103.1 1.0 fusion.1
  104.2 1.3 %fusion.2 = f32[4,8,64]{2,1,0:T(8,128)S(1)} fusion(f32[4,512,64,8]{1,2,3,0:T(8,128)S(1)} %get-tuple-element.46, f32[4,8,64]{2,1,0:T(8,128)S(1)} %get-tuple-element.31, pred[64,512]{1,0:T(8,128)(4,1)S(1)} %fusion.16), kind=kLoop, calls=%fused_computation.6 | loop fusion | flops 5240832 | bytes 4243456 | tf_op jit(solution)/shard_map/while/body/eval_jaxpr/reduce_sum | solution.py:147
  105.5 1.6 %fusion.19 = bf16[64,4,8,128]{3,0,2,1:T(8,128)(2,1)S(1)} fusion(f32[4,512,64,8]{1,2,3,0:T(8,128)S(1)} %get-tuple-element.46, f32[4,8,64]{2,1,0:T(8,128)S(1)} %get-tuple-element.31, pred[64,512]{1,0:T(8,128)(4,1)S(1)} %fusion.16, bf16[512,4,128,1]{2,1,0,3:T(4,128)(2,1)S(1)} %bitcast.74, f32[64,4,8]{0,2,1:T(8,128)S(1)} %bitcast_add_fusion, ...), kind=kOutput, calls=%fused_computation.28 | convolution fusion | flops 273416192 | bytes 5300224 | tf_op jit(solution)/shard_map/while/body/eval_jaxpr/hgqk,khd->hgqd/dot_general | solution.py:148
  107.1 0.3 copy.36
  107.5 0.2 reshape.294
  107.7 1.0 select_convert_fusion
  (19 shorter events, 0.2 us)
Async XLA Ops:
  7.2 22.1 %copy-start = (bf16[2048,128]{1,0:T(8,128)(2,1)S(1)}, bf16[2048,128]{1,0:T(8,128)(2,1)}, u32[]{:S(2)}) copy-start(bf16[2048,128]{1,0:T(8,128)(2,1)} %param.11) | copy-start | bytes 1572868
  10.6 18.7 %all-to-all-start = ((bf16[64,4,2048]{2,0,1:T(8,128)(2,1)}), bf16[64,4,2048]{2,0,1:T(8,128)(2,1)S(1)}, u32[]{:S(2)}, u32[]{:S(2)}) async-start(bf16[64,4,2048]{2,0,1:T(8,128)(2,1)} %copy.31), calls=%async_computation | async-start | bytes 2097152 | tf_op jit(solution)/shard_map/all_to_all | solution.py:80
  14.8 42.6 %reduce-scatter.2.cloned.1.call-start = ((), (), s32[]{:S(2)}) async-start(), calls=%async_computation.3 | async-start | bytes 737280 | tf_op jit(solution)/shard_map/reduce_scatter | solution.py:81
  29.7 5.2 %copy-start.3 = (s32[4,16]{1,0:T(4,128)S(1)}, s32[4,16]{1,0:T(4,128)}, u32[]{:S(2)}) copy-start(s32[4,16]{1,0:T(4,128)} %param.15) | copy-start | bytes 772
  29.8 28.6 %copy-start.2 = (bf16[2,64,512]{2,1,0:T(8,128)(2,1)S(1)}, bf16[2,64,512]{2,1,0:T(8,128)(2,1)}, u32[]{:S(2)}) copy-start(bf16[2,64,512]{2,1,0:T(8,128)(2,1)} %param.12) | copy-start | bytes 393220
  29.8 31.5 %copy-start.1 = (bf16[1,64,4096]{2,1,0:T(8,128)(2,1)S(1)}, bf16[1,64,4096]{2,1,0:T(8,128)(2,1)}, u32[]{:S(2)}) copy-start(bf16[1,64,4096]{2,1,0:T(8,128)(2,1)} %param.9) | copy-start | bytes 1572868
  33.3 28.5 %copy-start.4 = (s32[1,4,4]{2,1,0:T(4,128)S(1)}, s32[1,4,4]{2,1,0:T(4,128)}, u32[]{:S(2)}) copy-start(s32[1,4,4]{2,1,0:T(4,128)} %param.13) | copy-start | bytes 196
  34.2 67.4 %all-gather.2.cloned.1.call-start = ((), (), s32[]{:S(2)}) async-start(), calls=%async_computation.4 | async-start | bytes 1179648 | tf_op jit(solution)/shard_map/all_gather | solution.py:119
  64.1 7.9 %all-to-all-start.1 = ((bf16[4,4,4096]{2,1,0:T(4,128)(2,1)}), bf16[4,4,4096]{2,1,0:T(4,128)(2,1)S(1)}, u32[]{:S(2)}, u32[]{:S(2)}) async-start(bf16[4,4,4096]{2,1,0:T(4,128)(2,1)} %convolution_convert_fusion), calls=%async_computation.2 | async-start | bytes 262144 | tf_op jit(solution)/shard_map/all_to_all | solution.py:47
Sparse Core Ops, SparseCore 0:
  34.3 23.0 reduce-scatter.1
  61.3 40.2 all-gather.1
where the time goes:
time: 116 us; the launch traced here: 115 us
  waiting for transfers between devices  69.7 us (60%)
  between operations  15 us (13%)
  matrix products  9.79 us (8%)
  starting transfers between devices  7.58 us (7%)
  local copies, waits for them, and re-layouts  7.46 us (6%)
  other arithmetic  5.95 us (5%)
    all_gather x1, waiting for transfers between devices, local(): piece = lax.all_gather(own, 'ctx', axis=0, tiled=True)  28.6 us
    reduce_scatter x1, waiting for transfers between devices, local(): lax.psum_scatter(jnp.concatenate([jnp.dot(mixed_output, key_value_weight,...  22 us
    all_to_all x1, waiting for transfers between devices, local(): lax.all_to_all(tokens[0], 'grp', split_axis=1, concat_axis=0, tiled=True)  14.4 us
    all_to_all x1, waiting for transfers between devices, send_pages(): lax.all_to_all(outgoing, 'grp', split_axis=0, concat_axis=0, tiled=True)  4.58 us
    all_to_all x1, starting transfers between devices, local(): lax.all_to_all(tokens[0], 'grp', split_axis=1, concat_axis=0, tiled=True)  4.21 us
    dot_general x1, matrix products, local(): jnp.dot(mixed_output, key_value_weight, preferred_element_type=jnp.float32)  3.5 us
    all_to_all x2, local copies, waits for them, and re-layouts, local(): lax.all_to_all(tokens[0], 'grp', split_axis=1, concat_axis=0, tiled=True)  3.45 us
    all_to_all x1, starting transfers between devices, send_pages(): lax.all_to_all(outgoing, 'grp', split_axis=0, concat_axis=0, tiled=True)  3.33 us
  transfers between devices with their start and end apart: 4, of which 4 were waited for; matrix products, arithmetic and copies ran while one was open for 4% of the time, Pallas kernels for 0%

commit v1 on v0

v1 whole, which is shorter than its diff:
```python
import functools
import math

import jax
import jax.numpy as jnp
from jax import lax
from jax.experimental import pallas as pl
from jax.experimental.pallas import tpu as pltpu
from jax.sharding import PartitionSpec as P

HEAD_SIZE = 128
HQ = 32
KEY_VALUE_HEADS = 4
PAGE = 4
TILE = 128
THETA = 500000.0
ADAPTER_SCALE = 0.5
CHUNKS = 2
MESH = pl.DeviceIdType.MESH
F32 = jnp.float32
BF16 = jnp.bfloat16


def iota(shape, axis):
    return lax.broadcasted_iota(jnp.int32, shape, axis)


def page_rows(table, ppd):
    eye = iota((ppd, ppd), 0) == iota((ppd, ppd), 1)
    dest = lax.div(table, ppd)
    slot = lax.rem(table, ppd)
    wide = jnp.broadcast_to(dest.astype(F32), (ppd, ppd))
    column = jnp.sum(jnp.where(eye, wide, 0.0), axis=1, keepdims=True)
    same = wide == column
    lane_later = iota((ppd, ppd), 1) > iota((ppd, ppd), 0)
    lane_earlier = iota((ppd, ppd), 1) < iota((ppd, ppd), 0)
    order_row = jnp.sum(jnp.where(same & lane_later, 1.0, 0.0), axis=0, keepdims=True)
    order_col = jnp.sum(jnp.where(same & lane_earlier, 1.0, 0.0), axis=1, keepdims=True)
    return dest, slot, order_row, order_col


def kernel(
    groups, nz, ny,
    tokens, queries, kvw, dw, up, mask, lengths, table,
    att_out, cache_out,
    wbuf, qbuf, xbuf, part, rbuf, kv, pout, pin, pickp, placep, bias, cosb, sinb, mst, lst, acc,
    wsem, qsem, osem, xs, xr, rs, rr, zs, ys, ls, kr, ps, pr,
):
    me = lax.axis_index("grp")
    ctx = lax.axis_index("ctx")
    z = ctx // ny
    y = ctx % ny
    tok = qbuf.shape[0]
    ck = tok // CHUNKS
    width = xbuf.shape[3]
    cols = kvw.shape[1]
    half = cols // 2
    ppd = tok // PAGE
    most = max(2, -(-ppd // groups))
    rows = most * PAGE
    nctx = nz * ny
    per = HQ // KEY_VALUE_HEADS

    def partner(j):
        p = me
        for b in range(groups.bit_length()):
            if (j >> b) & 1:
                p = p + (1 << b) * (1 - 2 * ((me // (1 << b)) % 2))
        return p

    barrier = pltpu.get_barrier_semaphore()
    for j in range(1, groups):
        pl.semaphore_signal(barrier, inc=1, device_id={"grp": partner(j)}, device_id_type=MESH)
    for d in range(1, nz):
        pl.semaphore_signal(barrier, inc=1, device_id={"ctx": ((z + d) % nz) * ny + y}, device_id_type=MESH)
    for d in range(1, ny):
        pl.semaphore_signal(barrier, inc=1, device_id={"ctx": z * ny + (y + d) % ny}, device_id_type=MESH)

    wcopies = [
        pltpu.make_async_copy(kvw, wbuf.at[:, pl.ds(0, cols)], wsem.at[0]),
        pltpu.make_async_copy(dw, wbuf.at[:, pl.ds(cols, dw.shape[1])], wsem.at[1]),
    ]
    qcopy = pltpu.make_async_copy(queries.at[0], qbuf, qsem)
    ocopies = [
        pltpu.make_async_copy(
            tokens.at[0, pl.ds(c * ck, ck), pl.ds(pl.multiple_of(me * width, 128), width)],
            xbuf.at[c, 0], osem.at[c])
        for c in range(CHUNKS)
    ]

    def xcopy(c, j):
        other = partner(j)
        return pltpu.make_async_remote_copy(
            src_ref=tokens.at[0, pl.ds(c * ck, ck), pl.ds(pl.multiple_of(other * width, 128), width)],
            dst_ref=xbuf.at[c, j], send_sem=xs.at[c, j], recv_sem=xr.at[c, j],
            device_id={"grp": other}, device_id_type=MESH)

    def rcopy(c, j):
        return pltpu.make_async_remote_copy(
            src_ref=part.at[c, j], dst_ref=rbuf.at[c, j], send_sem=rs.at[c, j], recv_sem=rr.at[c, j],
            device_id={"grp": partner(j)}, device_id_type=MESH)

    def kcopy(c, source, target, send):
        return pltpu.make_async_remote_copy(
            src_ref=kv.at[c, source], dst_ref=kv.at[c, source], send_sem=send, recv_sem=kr.at[c, source],
            device_id={"ctx": target}, device_id_type=MESH)

    def pcopy(j):
        return pltpu.make_async_remote_copy(
            src_ref=pout.at[pl.ds(j * rows, rows)], dst_ref=pin.at[pl.ds(j * rows, rows)],
            send_sem=ps.at[j], recv_sem=pr.at[j],
            device_id={"grp": partner(j)}, device_id_type=MESH)

    pl.semaphore_wait(barrier, groups - 1 + nz - 1 + ny - 1)
    order = list(range(2, groups)) + [1]
    for c in range(CHUNKS):
        for j in order:
            xcopy(c, j).start()
    for copy in ocopies + wcopies + [qcopy]:
        copy.start()

    lane = iota((tok, HEAD_SIZE), 1)
    pair = lax.rem(lane, HEAD_SIZE // 2).astype(F32)
    freq = jnp.exp(pair * (-2.0 * math.log(THETA) / HEAD_SIZE))
    angle = (ctx * tok + iota((tok, HEAD_SIZE), 0)).astype(F32) * freq
    cosb[...] = jnp.cos(angle)
    sinb[...] = jnp.where(lane < HEAD_SIZE // 2, -1.0, 1.0) * jnp.sin(angle)

    length = lengths[0]
    qtile = (ctx * tok) // TILE
    n = nctx * ck
    for c in range(CHUNKS):
        lanes = iota((1, n), 1)
        kpos = lax.div(lanes, ck) * tok + c * ck + lax.rem(lanes, ck)
        ktile = lax.div(kpos, TILE)
        live = ktile == qtile
        for t in range(mask.shape[1]):
            live = live | ((ktile == t) & (mask[0, qtile, t] > 0))
        live = live & (kpos < length)
        qpos = ctx * tok + iota((tok, n), 0)
        later = jnp.broadcast_to(jnp.where(live, kpos, 1 << 30), (tok, n))
        same = jnp.broadcast_to(kpos, (tok, n)) == qpos
        bias[c] = jnp.where((later <= qpos) | same, 0.0, -1e30)

    @pl.loop(0, nctx)
    def _(s):
        @pl.when(s > ctx)
        def _():
            for c in range(CHUNKS):
                kv[c, s] = jnp.zeros((ck, cols), BF16)

    dest, slot, order_row, _ = page_rows(table[pl.ds(me, 1), :], ppd)
    r = iota((groups * rows, ppd), 0)
    target = lax.div(r, rows) ^ me
    nth = lax.div(lax.rem(r, rows), PAGE).astype(F32)
    chosen = jnp.where((jnp.broadcast_to(dest, r.shape) == target) & (order_row == nth), 1.0, 0.0)
    spread = jnp.where(lax.div(iota((ppd, tok), 1), PAGE) == iota((ppd, tok), 0), 1.0, 0.0)
    pick = jnp.dot(chosen.astype(BF16), spread.astype(BF16), preferred_element_type=F32)
    shape = (groups * rows, tok)
    line = lax.rem(iota(shape, 0), PAGE) == lax.rem(iota(shape, 1), PAGE)
    pickp[...] = jnp.where(line, pick, 0.0).astype(BF16)

    place = jnp.zeros((tok, groups * rows), F32)
    for j in range(groups):
        dest, slot, _, order_col = page_rows(table[pl.ds(partner(j), 1), :], ppd)
        o = lax.div(iota((tok, ppd), 0), PAGE)
        here = jnp.where((jnp.broadcast_to(slot, o.shape) == o) & (jnp.broadcast_to(dest, o.shape) == me), 1.0, 0.0)
        i = iota((ppd, groups * rows), 1)
        nth = lax.div(lax.rem(i, rows), PAGE).astype(F32)
        there = jnp.where((lax.div(i, rows) == j) & (order_col == nth), 1.0, 0.0)
        place = place + jnp.dot(here.astype(BF16), there.astype(BF16), preferred_element_type=F32)
    shape = (tok, groups * rows)
    line = lax.rem(iota(shape, 0), PAGE) == lax.rem(iota(shape, 1), PAGE)
    placep[...] = jnp.where(line, place, 0.0).astype(BF16)

    def project(c, first, last):
        x = xbuf[c, first:last].reshape((last - first) * ck, width)
        term = jnp.dot(x, wbuf[...], preferred_element_type=F32).astype(BF16)
        part[c, first:last] = term.reshape(last - first, ck, term.shape[1])
        for j in range(first, last):
            if j:
                rcopy(c, j).start()

    for copy in ocopies + wcopies:
        copy.wait()
    for c in range(CHUNKS):
        xcopy(c, 1).wait_recv()
        project(c, 0, 2)
    for c in range(CHUNKS):
        for j in range(2, groups):
            xcopy(c, j).wait_recv()
        project(c, 2, groups)

    for c in range(CHUNKS):
        total = part[c, 0].astype(F32)
        for j in range(1, groups):
            rcopy(c, j).wait_recv()
            total = total + rbuf[c, j].astype(F32)
        low = total[:, cols:].astype(BF16)
        first = iota(low.shape, 1) < low.shape[1] // 2
        none = jnp.zeros_like(low)
        keys = total[:, :half] + ADAPTER_SCALE * jnp.dot(
            jnp.where(first, low, none), up[...], preferred_element_type=F32)
        values = total[:, half:cols] + ADAPTER_SCALE * jnp.dot(
            jnp.where(first, none, low), up[...], preferred_element_type=F32)
        cosine = cosb[pl.ds(c * ck, ck), :]
        sine = sinb[pl.ds(c * ck, ck), :]
        for h in range(KEY_VALUE_HEADS):
            k = keys[:, h * HEAD_SIZE:(h + 1) * HEAD_SIZE]
            k = k * cosine + pltpu.roll(k, HEAD_SIZE // 2, 1) * sine
            kv[c, ctx, :, pl.ds(h * HEAD_SIZE, HEAD_SIZE)] = k.astype(BF16)
        kv[c, ctx, :, pl.ds(half, half)] = values.astype(BF16)
        for d in range(1, nz):
            @pl.when(z + d < nz)
            def _():
                kcopy(c, ctx, ctx + d * ny, zs.at[c, d]).start()
        for d in range(1, ny):
            @pl.when(y + d < ny)
            def _():
                kcopy(c, ctx, ctx + d, ys.at[c, d]).start()

    own = jnp.concatenate([kv[c, ctx] for c in range(CHUNKS)], axis=0)
    pout[...] = jnp.dot(pickp[...], own, preferred_element_type=F32).astype(BF16)
    for j in range(1, groups):
        pcopy(j).start()
    pin[pl.ds(0, rows), :] = pout[pl.ds(0, rows), :]
    qcopy.wait()

    scale = 1.0 / HEAD_SIZE**0.5
    for c in range(CHUNKS):
        for d in range(1, nz):
            @pl.when(d <= z)
            def _():
                source = ctx - d * ny
                kcopy(c, source, z * ny + (y + 1) % ny, ls.at[c, d, 1]).wait_recv()
                for e in range(1, ny):
                    kcopy(c, source, z * ny + (y + e) % ny, ls.at[c, d, e]).start()
        for d in range(1, ny):
            other = (y + d) % ny
            @pl.when(other < y)
            def _():
                kcopy(c, z * ny + other, z * ny + other, ys.at[c, d]).wait_recv()
            for e in range(1, nz):
                @pl.when(e <= z)
                def _():
                    kcopy(c, (z - e) * ny + other, z * ny + other, ls.at[c, e, d]).wait_recv()

        for h in range(KEY_VALUE_HEADS):
            q = jnp.concatenate(
                [qbuf[:, pl.ds((h * per + g) * HEAD_SIZE, HEAD_SIZE)] for g in range(per)], axis=0)
            k = kv[c, :, :, pl.ds(h * HEAD_SIZE, HEAD_SIZE)].reshape(n, HEAD_SIZE)
            v = kv[c, :, :, pl.ds(half + h * HEAD_SIZE, HEAD_SIZE)].reshape(n, HEAD_SIZE)
            s = lax.dot_general(q, k, (((1,), (1,)), ((), ())), preferred_element_type=F32) * scale
            s = (s.reshape(per, tok, n) + bias[c][None]).reshape(per * tok, n)
            peak = jnp.max(s, axis=1, keepdims=True)
            if c:
                before = mst[h]
                peak = jnp.maximum(peak, before)
            e = jnp.exp(s - peak)
            total = jnp.sum(e, axis=1, keepdims=True)
            out = jnp.dot(e.astype(BF16), v, preferred_element_type=F32)
            if c:
                factor = jnp.exp(before - peak)
                total = total + lst[h] * factor
                out = out + acc[h] * factor
            if c < CHUNKS - 1:
                mst[h] = peak
                lst[h] = total
                acc[h] = out
            else:
                out = out / total
                alive = ctx * tok + iota((tok, HEAD_SIZE), 0) < length
                for g in range(per):
                    piece = jnp.where(alive, out[g * tok:(g + 1) * tok], 0.0)
                    att_out[0, :, pl.ds((h * per + g) * HEAD_SIZE, HEAD_SIZE)] = piece.astype(BF16)
        if c == 0:
            for j in range(1, groups):
                pcopy(j).wait_recv()
            cache_out[...] = jnp.dot(placep[...], pin[...], preferred_element_type=F32).astype(BF16)

    for c in range(CHUNKS):
        for j in range(1, groups):
            xcopy(c, j).wait_send()
            rcopy(c, j).wait_send()
        for d in range(1, nz):
            @pl.when(z + d < nz)
            def _():
                kcopy(c, ctx, ctx + d * ny, zs.at[c, d]).wait_send()
            @pl.when(d <= z)
            def _():
                for e in range(1, ny):
                    kcopy(c, ctx - d * ny, z * ny + (y + e) % ny, ls.at[c, d, e]).wait_send()
        for d in range(1, ny):
            @pl.when(y + d < ny)
            def _():
                kcopy(c, ctx, ctx + d, ys.at[c, d]).wait_send()
    for j in range(1, groups):
        pcopy(j).wait_send()


def local(nctx, groups, tokens, queries, kvw, dw, up, mask, lengths, table):
    ny = 1
    while ny * ny * 4 <= nctx and nctx % (ny * 2) == 0:
        ny *= 2
    nz = nctx // ny
    tok = tokens.shape[1]
    ck = tok // CHUNKS
    width, cols = kvw.shape
    full = cols + dw.shape[1]
    ppd = tok // PAGE
    rows = max(2, -(-ppd // groups)) * PAGE
    per = HQ // KEY_VALUE_HEADS
    n = nctx * ck
    dma = pltpu.SemaphoreType.DMA
    hbm = pl.BlockSpec(memory_space=pl.ANY)
    vmem = pl.BlockSpec(memory_space=pltpu.VMEM)
    smem = pl.BlockSpec(memory_space=pltpu.SMEM)
    attended, cache = pl.pallas_call(
        functools.partial(kernel, groups, nz, ny),
        out_shape=(
            jax.ShapeDtypeStruct(queries.shape, BF16),
            jax.ShapeDtypeStruct((tok, cols), BF16),
        ),
        in_specs=[hbm, hbm, hbm, hbm, vmem, smem, smem, vmem],
        out_specs=(vmem, vmem),
        scratch_shapes=[
            pltpu.VMEM((width, full), BF16),
            pltpu.VMEM((tok, HQ * HEAD_SIZE), BF16),
            pltpu.VMEM((CHUNKS, groups, ck, width), BF16),
            pltpu.VMEM((CHUNKS, groups, ck, full), BF16),
            pltpu.VMEM((CHUNKS, groups, ck, full), BF16),
            pltpu.VMEM((CHUNKS, nctx, ck, cols), BF16),
            pltpu.VMEM((groups * rows, cols), BF16),
            pltpu.VMEM((groups * rows, cols), BF16),
            pltpu.VMEM((groups * rows, tok), BF16),
            pltpu.VMEM((tok, groups * rows), BF16),
            pltpu.VMEM((CHUNKS, tok, n), F32),
            pltpu.VMEM((tok, HEAD_SIZE), F32),
            pltpu.VMEM((tok, HEAD_SIZE), F32),
            pltpu.VMEM((KEY_VALUE_HEADS, per * tok, 1), F32),
            pltpu.VMEM((KEY_VALUE_HEADS, per * tok, 1), F32),
            pltpu.VMEM((KEY_VALUE_HEADS, per * tok, HEAD_SIZE), F32),
            dma((2,)),
            dma,
            dma((CHUNKS,)),
            dma((CHUNKS, groups)),
            dma((CHUNKS, groups)),
            dma((CHUNKS, groups)),
            dma((CHUNKS, groups)),
            dma((CHUNKS, nz)),
            dma((CHUNKS, ny)),
            dma((CHUNKS, nz, ny)),
            dma((CHUNKS, nctx)),
            dma((groups,)),
            dma((groups,)),
        ],
        compiler_params=pltpu.CompilerParams(
            collective_id=0, has_side_effects=True, vmem_limit_bytes=56 * 1024 * 1024
        ),
    )(tokens, queries, kvw, dw, up.reshape(-1, up.shape[2]), mask, lengths, table)
    return attended, cache.reshape(1, ppd, PAGE, cols)


def solution(mesh):
    in_specs = (
        P("grp", "ctx", None),
        P("grp", "ctx", None),
        P("grp", None),
        P("grp", None),
        P(),
        P("grp", None, None),
        P("grp"),
        P(None, "ctx"),
    )
    out_specs = (P("grp", "ctx", None), P("grp", "ctx", None, None))
    body = functools.partial(local, mesh.shape["ctx"], mesh.shape["grp"])
    return jax.shard_map(body, mesh=mesh, in_specs=in_specs, out_specs=out_specs, check_vma=False)
```

time: 116 us -> 48.2 us (0.42)
  the two profiles are of different devices: /device:TPU:0 before, /device:TPU:24 now
where the time goes in v1:
time: 48.2 us; the launch traced here: 48 us
  Pallas kernels  43.2 us (90%)
  local copies, waits for them, and re-layouts  3.48 us (7%)
  between operations  1.29 us (3%)
    pallas_call x1, Pallas kernels, local(): pl.pallas_call(functools.partial(kernel, groups, nz, ny), out_shape=(jax....  43.2 us
    unnamed x1, local copies, waits for them, and re-layouts  1.87 us
    reshape x1, local copies, waits for them, and re-layouts, local(): return (attended, cache.reshape(1, ppd, PAGE, cols))  1.62 us

profile of v1, /device:TPU:24, one launch (start us, length us, event | category | flops | bytes accessed | tf_op | source)
XLA Modules:
  0.0 48.0 jit_solution(3466968746441976492)
XLA Ops:
  1.3 43.2 %shard_map.95 = (bf16[1,64,4096]{2,1,0:T(8,128)(2,1)}, bf16[64,1024]{1,0:T(8,128)(2,1)}) custom-call(bf16[1,64,8192]{2,1,0:T(8,128)(2,1)} %tokens.1, bf16[1,64,4096]{2,1,0:T(8,128)(2,1)} %queries.1, bf16[2048,1024]{1,0:T(8,128)(2,1)} %kvw.1, bf16[2048,128]{1,0:T(8,128)(2,1)} %dw.1, bf16[128,512]{1,0:T(8,128)(2,1)} %bitcast.1, s32[1,4,4]{2,1,0:T(4,128)} %mask.1, ...), custom_call_target="tpu_custom_call" | custom-call | tf_op jit(solution)/shard_map/pallas_call | solution.py:318
  44.5 1.6 %reshape.11 = bf16[1,16,4,1024]{3,2,1,0:T(4,128)(2,1)} reshape(bf16[64,1024]{1,0:T(8,128)(2,1)} %get-tuple-element.5) | data formatting | bytes 262144 | tf_op jit(solution)/shard_map/reshape | solution.py:361
  46.1 1.9 %copy.12 = bf16[1,64,4096]{2,1,0:T(8,128)(2,1)} copy(bf16[1,64,4096]{2,1,0:T(8,128)(2,1)} %get-tuple-element.8) | data formatting | bytes 1048576

commit v2 on v1

v2 whole, which is shorter than its diff:
```python
import functools
import math

import jax
import jax.numpy as jnp
from jax import lax
from jax.experimental import pallas as pl
from jax.experimental.pallas import tpu as pltpu
from jax.sharding import PartitionSpec as P

HEAD_SIZE = 128
HQ = 32
KEY_VALUE_HEADS = 4
PAGE = 4
TILE = 128
THETA = 500000.0
ADAPTER_SCALE = 0.5
CHUNKS = 4
DEPTH = 2
SPANS = ((0, 3), (3, 4))
MESH = pl.DeviceIdType.MESH
F32 = jnp.float32
BF16 = jnp.bfloat16


def iota(shape, axis):
    return lax.broadcasted_iota(jnp.int32, shape, axis)


def page_rows(table, ppd):
    eye = iota((ppd, ppd), 0) == iota((ppd, ppd), 1)
    dest = lax.div(table, ppd)
    slot = lax.rem(table, ppd)
    wide = jnp.broadcast_to(dest.astype(F32), (ppd, ppd))
    column = jnp.sum(jnp.where(eye, wide, 0.0), axis=1, keepdims=True)
    same = wide == column
    lane_later = iota((ppd, ppd), 1) > iota((ppd, ppd), 0)
    lane_earlier = iota((ppd, ppd), 1) < iota((ppd, ppd), 0)
    order_row = jnp.sum(jnp.where(same & lane_later, 1.0, 0.0), axis=0, keepdims=True)
    order_col = jnp.sum(jnp.where(same & lane_earlier, 1.0, 0.0), axis=1, keepdims=True)
    return dest, slot, order_row, order_col


def kernel(
    groups, nz, ny,
    tokens, queries, kvw, dw, up, mask, lengths, table,
    att_out, cache_out,
    wbuf, qbuf, near, far, nearp, nearr, farp, cross, summed, farr, kv, pout, pin, pickp, placep, bias, cosb, sinb,
    mst, lst, acc,
    wsem, qsem, osem, ns, nr, ms, mr, xs, xr, cs, cr, rs, rr, zs, ys, ls, kr, ps, pr, ready,
):
    me = lax.axis_index("grp")
    ctx = lax.axis_index("ctx")
    z = ctx // ny
    y = ctx % ny
    tok = qbuf.shape[0]
    ck = tok // CHUNKS
    width = near.shape[2]
    pairs = groups // 2 - 1
    cols = kvw.shape[1]
    half = cols // 2
    ppd = tok // PAGE
    most = max(2, -(-ppd // groups))
    rows = most * PAGE
    nctx = nz * ny
    per = HQ // KEY_VALUE_HEADS

    def partner(j):
        p = me
        for b in range(groups.bit_length()):
            if (j >> b) & 1:
                p = p + (1 << b) * (1 - 2 * ((me // (1 << b)) % 2))
        return p

    barrier = pltpu.get_barrier_semaphore()
    for j in range(1, groups):
        pl.semaphore_signal(barrier, inc=1, device_id={"grp": partner(j)}, device_id_type=MESH)

    @pl.when(z > 0)
    def _():
        pl.semaphore_signal(barrier, inc=1, device_id={"ctx": ctx - ny}, device_id_type=MESH)

    @pl.when(z < nz - 1)
    def _():
        pl.semaphore_signal(barrier, inc=1, device_id={"ctx": ctx + ny}, device_id_type=MESH)

    for d in range(1, ny):
        pl.semaphore_signal(barrier, inc=1, device_id={"ctx": z * ny + (y + d) % ny}, device_id_type=MESH)

    wcopies = [
        pltpu.make_async_copy(kvw, wbuf.at[:, pl.ds(0, cols)], wsem.at[0]),
        pltpu.make_async_copy(dw, wbuf.at[:, pl.ds(cols, dw.shape[1])], wsem.at[1]),
    ]
    qcopy = pltpu.make_async_copy(queries.at[0], qbuf, qsem)
    ocopy = pltpu.make_async_copy(
        tokens.at[0, :, pl.ds(pl.multiple_of(me * width, 128), width)], near.at[0], osem)

    def ncopy():
        return pltpu.make_async_remote_copy(
            src_ref=tokens.at[0, :, pl.ds(pl.multiple_of(partner(1) * width, 128), width)],
            dst_ref=near.at[1], send_sem=ns, recv_sem=nr, device_id={"grp": partner(1)}, device_id_type=MESH)

    def mcopy():
        return pltpu.make_async_remote_copy(
            src_ref=nearp.at[1], dst_ref=nearr, send_sem=ms, recv_sem=mr,
            device_id={"grp": partner(1)}, device_id_type=MESH)

    def xcopy(c, j):
        other = partner(j)
        return pltpu.make_async_remote_copy(
            src_ref=tokens.at[0, pl.ds(c * ck, ck), pl.ds(pl.multiple_of(other * width, 128), width)],
            dst_ref=far.at[c, j - 2], send_sem=xs.at[c, j], recv_sem=xr.at[c, j],
            device_id={"grp": other}, device_id_type=MESH)

    def ccopy(c, k):
        return pltpu.make_async_remote_copy(
            src_ref=farp.at[c, 2 * k + 1], dst_ref=cross.at[c, k], send_sem=cs.at[c, k], recv_sem=cr.at[c, k],
            device_id={"grp": partner(1)}, device_id_type=MESH)

    def rcopy(c, k):
        return pltpu.make_async_remote_copy(
            src_ref=summed.at[c, k], dst_ref=farr.at[c, k], send_sem=rs.at[c, k], recv_sem=rr.at[c, k],
            device_id={"grp": partner(2 * k + 2)}, device_id_type=MESH)

    def kcopy(c, source, target, send):
        return pltpu.make_async_remote_copy(
            src_ref=kv.at[c, source], dst_ref=kv.at[c, source], send_sem=send, recv_sem=kr.at[c, source],
            device_id={"ctx": target}, device_id_type=MESH)

    def pcopy(j):
        return pltpu.make_async_remote_copy(
            src_ref=pout.at[pl.ds(j * rows, rows)], dst_ref=pin.at[pl.ds(j * rows, rows)],
            send_sem=ps.at[j], recv_sem=pr.at[j],
            device_id={"grp": partner(j)}, device_id_type=MESH)

    for copy in wcopies + [ocopy, qcopy]:
        copy.start()
    pl.semaphore_wait(barrier, groups - 1 + ny - 1 + jnp.where(z > 0, 1, 0) + jnp.where(z < nz - 1, 1, 0))
    for c in range(DEPTH):
        for j in range(2, groups):
            xcopy(c, j).start()
    ncopy().start()

    def tell_of(d):
        @pl.when((z > 0) & (z + d - 1 < nz))
        def _():
            pl.semaphore_signal(ready, inc=1, device_id={"ctx": ctx - ny}, device_id_type=MESH)

    tell_of(2)

    lane = iota((tok, HEAD_SIZE), 1)
    pair = lax.rem(lane, HEAD_SIZE // 2).astype(F32)
    freq = jnp.exp(pair * (-2.0 * math.log(THETA) / HEAD_SIZE))
    angle = (ctx * tok + iota((tok, HEAD_SIZE), 0)).astype(F32) * freq
    cosb[...] = jnp.cos(angle)
    sinb[...] = jnp.where(lane < HEAD_SIZE // 2, -1.0, 1.0) * jnp.sin(angle)

    length = lengths[0]
    qtile = (ctx * tok) // TILE
    n = nctx * ck
    for c in range(CHUNKS):
        lanes = iota((1, n), 1)
        kpos = lax.div(lanes, ck) * tok + c * ck + lax.rem(lanes, ck)
        ktile = lax.div(kpos, TILE)
        live = ktile == qtile
        for t in range(mask.shape[1]):
            live = live | ((ktile == t) & (mask[0, qtile, t] > 0))
        live = live & (kpos < length)
        qpos = ctx * tok + iota((tok, n), 0)
        later = jnp.broadcast_to(jnp.where(live, kpos, 1 << 30), (tok, n))
        same = jnp.broadcast_to(kpos, (tok, n)) == qpos
        bias[:, c * n:(c + 1) * n] = jnp.where((later <= qpos) | same, 0.0, -1e30)

    @pl.loop(0, nctx)
    def _(s):
        @pl.when(s > ctx)
        def _():
            for c in range(CHUNKS):
                kv[c, s] = jnp.zeros((ck, cols), BF16)

    for d in range(3, nz + 1):
        @pl.when(z + d - 1 < nz)
        def _():
            pl.semaphore_wait(ready, 1)
        tell_of(d)

    def page_tables():
        dest, slot, order_row, _ = page_rows(table[pl.ds(me, 1), :], ppd)
        r = iota((groups * rows, ppd), 0)
        target = lax.div(r, rows) ^ me
        nth = lax.div(lax.rem(r, rows), PAGE).astype(F32)
        chosen = jnp.where((jnp.broadcast_to(dest, r.shape) == target) & (order_row == nth), 1.0, 0.0)
        spread = jnp.where(lax.div(iota((ppd, tok), 1), PAGE) == iota((ppd, tok), 0), 1.0, 0.0)
        pick = jnp.dot(chosen.astype(BF16), spread.astype(BF16), preferred_element_type=F32)
        shape = (groups * rows, tok)
        line = lax.rem(iota(shape, 0), PAGE) == lax.rem(iota(shape, 1), PAGE)
        pickp[...] = jnp.where(line, pick, 0.0).astype(BF16)

        place = jnp.zeros((tok, groups * rows), F32)
        for j in range(groups):
            dest, slot, _, order_col = page_rows(table[pl.ds(partner(j), 1), :], ppd)
            o = lax.div(iota((tok, ppd), 0), PAGE)
            here = jnp.where((jnp.broadcast_to(slot, o.shape) == o) & (jnp.broadcast_to(dest, o.shape) == me), 1.0, 0.0)
            i = iota((ppd, groups * rows), 1)
            nth = lax.div(lax.rem(i, rows), PAGE).astype(F32)
            there = jnp.where((lax.div(i, rows) == j) & (order_col == nth), 1.0, 0.0)
            place = place + jnp.dot(here.astype(BF16), there.astype(BF16), preferred_element_type=F32)
        shape = (tok, groups * rows)
        line = lax.rem(iota(shape, 0), PAGE) == lax.rem(iota(shape, 1), PAGE)
        placep[...] = jnp.where(line, place, 0.0).astype(BF16)

    ocopy.wait()
    for copy in wcopies:
        copy.wait()
    ncopy().wait_recv()
    x = near[...].reshape(2 * tok, width)
    nearp[...] = jnp.dot(x, wbuf[...], preferred_element_type=F32).astype(BF16).reshape(nearp.shape)
    mcopy().start()

    def project(c):
        for j in range(2, groups):
            xcopy(c, j).wait_recv()
        if c + DEPTH < CHUNKS:
            for j in range(2, groups):
                xcopy(c, j).wait_send()
                xcopy(c + DEPTH, j).start()
        x = far[c].reshape(2 * pairs * ck, width)
        term = jnp.dot(x, wbuf[...], preferred_element_type=F32).astype(BF16)
        farp[c] = term.reshape(2 * pairs, ck, term.shape[1])
        for k in range(pairs):
            ccopy(c, k).start()

    def chip_sum(c):
        for k in range(pairs):
            ccopy(c, k).wait_recv()
            summed[c, k] = (farp[c, 2 * k].astype(F32) + cross[c, k].astype(F32)).astype(BF16)
            rcopy(c, k).start()

    def finish(c):
        if c == 0:
            mcopy().wait_recv()
        total = nearp[0, pl.ds(c * ck, ck), :].astype(F32) + nearr[pl.ds(c * ck, ck), :].astype(F32)
        for k in range(pairs):
            rcopy(c, k).wait_recv()
            total = total + farr[c, k].astype(F32)
        low = total[:, cols:].astype(BF16)
        first = iota(low.shape, 1) < low.shape[1] // 2
        none = jnp.zeros_like(low)
        keys = total[:, :half] + ADAPTER_SCALE * jnp.dot(
            jnp.where(first, low, none), up[...], preferred_element_type=F32)
        values = total[:, half:cols] + ADAPTER_SCALE * jnp.dot(
            jnp.where(first, none, low), up[...], preferred_element_type=F32)
        cosine = cosb[pl.ds(c * ck, ck), :]
        sine = sinb[pl.ds(c * ck, ck), :]
        for h in range(KEY_VALUE_HEADS):
            k = keys[:, h * HEAD_SIZE:(h + 1) * HEAD_SIZE]
            k = k * cosine + pltpu.roll(k, HEAD_SIZE // 2, 1) * sine
            kv[c, ctx, :, pl.ds(h * HEAD_SIZE, HEAD_SIZE)] = k.astype(BF16)
        kv[c, ctx, :, pl.ds(half, half)] = values.astype(BF16)
        for d in range(1, nz):
            @pl.when(z + d < nz)
            def _():
                kcopy(c, ctx, ctx + d * ny, zs.at[c, d]).start()
        for d in range(1, ny):
            @pl.when(y + d < ny)
            def _():
                kcopy(c, ctx, ctx + d, ys.at[c, d]).start()

    def relay(c):
        for d in range(1, nz):
            @pl.when(d <= z)
            def _():
                source = ctx - d * ny
                kcopy(c, source, z * ny + (y + 1) % ny, ls.at[c, d, 1]).wait_recv()
                for e in range(1, ny):
                    kcopy(c, source, z * ny + (y + e) % ny, ls.at[c, d, e]).start()

    def landed(c):
        for d in range(1, ny):
            other = (y + d) % ny
            @pl.when(other < y)
            def _():
                kcopy(c, z * ny + other, z * ny + other, ys.at[c, d]).wait_recv()
            for e in range(1, nz):
                @pl.when(e <= z)
                def _():
                    kcopy(c, (z - e) * ny + other, z * ny + other, ls.at[c, e, d]).wait_recv()

    def attend(i):
        first, last = SPANS[i]
        m = (last - first) * n
        for h in range(KEY_VALUE_HEADS):
            q = jnp.concatenate(
                [qbuf[:, pl.ds((h * per + g) * HEAD_SIZE, HEAD_SIZE)] for g in range(per)], axis=0)
            k = kv[first:last, :, :, pl.ds(h * HEAD_SIZE, HEAD_SIZE)].reshape(m, HEAD_SIZE)
            v = kv[first:last, :, :, pl.ds(half + h * HEAD_SIZE, HEAD_SIZE)].reshape(m, HEAD_SIZE)
            s = lax.dot_general(q, k, (((1,), (1,)), ((), ())), preferred_element_type=F32) * scale
            s = (s.reshape(per, tok, m) + bias[:, first * n:last * n][None]).reshape(per * tok, m)
            peak = jnp.max(s, axis=1, keepdims=True)
            if i:
                before = mst[h]
                peak = jnp.maximum(peak, before)
            e = jnp.exp(s - peak)
            total = jnp.sum(e, axis=1, keepdims=True)
            out = jnp.dot(e.astype(BF16), v, preferred_element_type=F32)
            if i:
                factor = jnp.exp(before - peak)
                total = total + lst[h] * factor
                out = out + acc[h] * factor
            if i < len(SPANS) - 1:
                mst[h] = peak
                lst[h] = total
                acc[h] = out
            else:
                out = out / total
                alive = ctx * tok + iota((tok, HEAD_SIZE), 0) < length
                for g in range(per):
                    piece = jnp.where(alive, out[g * tok:(g + 1) * tok], 0.0)
                    att_out[0, :, pl.ds((h * per + g) * HEAD_SIZE, HEAD_SIZE)] = piece.astype(BF16)
    length = lengths[0]
    scale = 1.0 / HEAD_SIZE**0.5
    page_tables()
    for c in range(CHUNKS):
        project(c)
        chip_sum(c)
        if c >= 1:
            finish(c - 1)
        if c >= 2:
            relay(c - 2)
    finish(CHUNKS - 1)

    own = jnp.concatenate([kv[c, ctx] for c in range(CHUNKS)], axis=0)
    pout[...] = jnp.dot(pickp[...], own, preferred_element_type=F32).astype(BF16)
    for j in range(1, groups):
        pcopy(j).start()
    pin[pl.ds(0, rows), :] = pout[pl.ds(0, rows), :]
    qcopy.wait()
    for c in range(CHUNKS - 2, SPANS[0][1]):
        relay(c)
    for i, (first, last) in enumerate(SPANS):
        if i == len(SPANS) - 1:
            for j in range(1, groups):
                pcopy(j).wait_recv()
            cache = jnp.dot(placep[...], pin[...], preferred_element_type=F32).astype(BF16)
            cache_out[0] = cache.reshape(cache_out.shape[1:])
        for c in range(max(first, CHUNKS - 2, SPANS[0][1]), last):
            relay(c)
        for c in range(first, last):
            landed(c)
        attend(i)

    for c in range(CHUNKS):
        for j in range(2, groups):
            if c + DEPTH >= CHUNKS:
                xcopy(c, j).wait_send()
        for k in range(pairs):
            ccopy(c, k).wait_send()
            rcopy(c, k).wait_send()
        for d in range(1, nz):
            @pl.when(z + d < nz)
            def _():
                kcopy(c, ctx, ctx + d * ny, zs.at[c, d]).wait_send()
            @pl.when(d <= z)
            def _():
                for e in range(1, ny):
                    kcopy(c, ctx - d * ny, z * ny + (y + e) % ny, ls.at[c, d, e]).wait_send()
        for d in range(1, ny):
            @pl.when(y + d < ny)
            def _():
                kcopy(c, ctx, ctx + d, ys.at[c, d]).wait_send()
    for j in range(1, groups):
        pcopy(j).wait_send()
    ncopy().wait_send()
    mcopy().wait_send()


def hand_over(attended, cache, attended_out, cache_out, first, second, sems):
    arrays = ((attended, first, attended_out), (cache, second, cache_out))
    into = [pltpu.make_async_copy(a, b, sems.at[0, i]) for i, (a, b, _) in enumerate(arrays)]
    back = [pltpu.make_async_copy(b, c, sems.at[1, i]) for i, (_, b, c) in enumerate(arrays)]
    for copy in into:
        copy.start()
    for a, b in zip(into, back):
        a.wait()
        b.start()
    for copy in back:
        copy.wait()


def local(nctx, groups, tokens, queries, kvw, dw, up, mask, lengths, table):
    ny = 1
    while ny * ny * 4 <= nctx and nctx % (ny * 2) == 0:
        ny *= 2
    nz = nctx // ny
    tok = tokens.shape[1]
    ck = tok // CHUNKS
    width, cols = kvw.shape
    full = cols + dw.shape[1]
    ppd = tok // PAGE
    rows = max(2, -(-ppd // groups)) * PAGE
    per = HQ // KEY_VALUE_HEADS
    n = nctx * ck
    pairs = groups // 2 - 1
    dma = pltpu.SemaphoreType.DMA
    hbm = pl.BlockSpec(memory_space=pl.ANY)
    vmem = pl.BlockSpec(memory_space=pltpu.VMEM)
    smem = pl.BlockSpec(memory_space=pltpu.SMEM)
    attended, cache = pl.pallas_call(
        functools.partial(kernel, groups, nz, ny),
        out_shape=(
            jax.ShapeDtypeStruct(queries.shape, BF16),
            jax.ShapeDtypeStruct((1, ppd, PAGE, cols), BF16),
        ),
        in_specs=[hbm, hbm, hbm, hbm, vmem, smem, smem, vmem],
        out_specs=(vmem, vmem),
        scratch_shapes=[
            pltpu.VMEM((width, full), BF16),
            pltpu.VMEM((tok, HQ * HEAD_SIZE), BF16),
            pltpu.VMEM((2, tok, width), BF16),
            pltpu.VMEM((CHUNKS, groups - 2, ck, width), BF16),
            pltpu.VMEM((2, tok, full), BF16),
            pltpu.VMEM((tok, full), BF16),
            pltpu.VMEM((CHUNKS, groups - 2, ck, full), BF16),
            pltpu.VMEM((CHUNKS, pairs, ck, full), BF16),
            pltpu.VMEM((CHUNKS, pairs, ck, full), BF16),
            pltpu.VMEM((CHUNKS, pairs, ck, full), BF16),
            pltpu.VMEM((CHUNKS, nctx, ck, cols), BF16),
            pltpu.VMEM((groups * rows, cols), BF16),
            pltpu.VMEM((groups * rows, cols), BF16),
            pltpu.VMEM((groups * rows, tok), BF16),
            pltpu.VMEM((tok, groups * rows), BF16),
            pltpu.VMEM((tok, CHUNKS * n), F32),
            pltpu.VMEM((tok, HEAD_SIZE), F32),
            pltpu.VMEM((tok, HEAD_SIZE), F32),
            pltpu.VMEM((KEY_VALUE_HEADS, per * tok, 1), F32),
            pltpu.VMEM((KEY_VALUE_HEADS, per * tok, 1), F32),
            pltpu.VMEM((KEY_VALUE_HEADS, per * tok, HEAD_SIZE), F32),
            dma((2,)),
            dma,
            dma,
            dma,
            dma,
            dma,
            dma,
            dma((CHUNKS, groups)),
            dma((CHUNKS, groups)),
            dma((CHUNKS, pairs)),
            dma((CHUNKS, pairs)),
            dma((CHUNKS, pairs)),
            dma((CHUNKS, pairs)),
            dma((CHUNKS, nz)),
            dma((CHUNKS, ny)),
            dma((CHUNKS, nz, ny)),
            dma((CHUNKS, nctx)),
            dma((groups,)),
            dma((groups,)),
            pltpu.SemaphoreType.REGULAR,
        ],
        compiler_params=pltpu.CompilerParams(
            collective_id=0, has_side_effects=True, vmem_limit_bytes=56 * 1024 * 1024
        ),
    )(tokens, queries, kvw, dw, up.reshape(-1, up.shape[2]), mask, lengths, table)
    return pl.pallas_call(
        hand_over,
        out_shape=(
            jax.ShapeDtypeStruct(attended.shape, BF16),
            jax.ShapeDtypeStruct(cache.shape, BF16),
        ),
        in_specs=[hbm, hbm],
        out_specs=(hbm, hbm),
        scratch_shapes=[pltpu.VMEM(attended.shape, BF16), pltpu.VMEM(cache.shape, BF16), dma((2, 2))],
    )(attended, cache)


def solution(mesh):
    in_specs = (
        P("grp", "ctx", None),
        P("grp", "ctx", None),
        P("grp", None),
        P("grp", None),
        P(),
        P("grp", None, None),
        P("grp"),
        P(None, "ctx"),
    )
    out_specs = (P("grp", "ctx", None), P("grp", "ctx", None, None))
    body = functools.partial(local, mesh.shape["ctx"], mesh.shape["grp"])
    return jax.shard_map(body, mesh=mesh, in_specs=in_specs, out_specs=out_specs, check_vma=False)
```

time: 48.2 us -> 42.4 us (0.88)
  local copies, waits for them, and re-layouts: 3.48 us -> 0 us
  Pallas kernels: 43.2 us -> 41 us
    pallas_call x1, Pallas kernels: 43.2 us -> 39.1 us  [local(): pl.pallas_call(functools.partial(kernel, groups, nz, ny), out_shape=(jax....]
    pallas_call x0 -> x1, Pallas kernels: none -> 1.9 us  [local(): pl.pallas_call(hand_over, out_shape=(jax.ShapeDtypeStruct(attended.shape,...]
    unnamed x1 -> x0, local copies, waits for them, and re-layouts: 1.87 us -> none
    reshape x1 -> x0, local copies, waits for them, and re-layouts: 1.62 us -> none  [local(): return (attended, cache.reshape(1, ppd, PAGE, cols))]
where the time goes in v2:
time: 42.4 us; the launch traced here: 42.2 us
  Pallas kernels  41 us (97%)
  between operations  1.29 us (3%)
    pallas_call x1, Pallas kernels, local(): pl.pallas_call(functools.partial(kernel, groups, nz, ny), out_shape=(jax....  39.1 us
    pallas_call x1, Pallas kernels, local(): pl.pallas_call(hand_over, out_shape=(jax.ShapeDtypeStruct(attended.shape,...  1.9 us

profile of v2, /device:TPU:24, one launch (start us, length us, event | category | flops | bytes accessed | tf_op | source)
XLA Modules:
  0.0 42.2 jit_solution(11052673284032161135)
XLA Ops:
  1.3 39.1 %shard_map.95 = (bf16[1,64,4096]{2,1,0:T(8,128)(2,1)}, bf16[1,16,4,1024]{3,2,1,0:T(4,128)(2,1)}) custom-call(bf16[1,64,8192]{2,1,0:T(8,128)(2,1)} %tokens.1, bf16[1,64,4096]{2,1,0:T(8,128)(2,1)} %queries.1, bf16[2048,1024]{1,0:T(8,128)(2,1)} %kvw.1, bf16[2048,128]{1,0:T(8,128)(2,1)} %dw.1, bf16[128,512]{1,0:T(8,128)(2,1)} %bitcast.1, s32[1,4,4]{2,1,0:T(4,128)} %mask.1, ...), custom_call_target="tpu_custom_call" | custom-call | tf_op jit(solution)/shard_map/pallas_call | solution.py:408
  40.3 1.9 %shard_map.96 = (bf16[1,64,4096]{2,1,0:T(8,128)(2,1)}, bf16[1,16,4,1024]{3,2,1,0:T(4,128)(2,1)}) custom-call(bf16[1,64,4096]{2,1,0:T(8,128)(2,1)} %get-tuple-element.4.attended, bf16[1,16,4,1024]{3,2,1,0:T(4,128)(2,1)} %get-tuple-element.5.cache), custom_call_target="tpu_custom_call" | custom-call | tf_op jit(solution)/shard_map/pallas_call | solution.py:463
